TPU v7x, 32 devices: a whole 2x2x4 slice. The times are simulated.
32 devices in a mesh: branch: 2 (over core), dp: 16 (over z, y, x).
Axes of the slice: x: 2, y: 2, z: 4, core: 2. Of those that a mesh axis runs over, the one named last changes fastest.
Arguments:
- small_tokens: bfloat16 [2, 128, 145, 192], P('branch', 'dp'), may hold values from -6 to 6
- large_tokens: bfloat16 [2, 128, 197, 384], P('branch', 'dp'), may hold values from -6 to 6
- small_cot: bfloat16 [2, 128, 145, 192], P('branch', 'dp'), may hold values from -6 to 6
- large_cot: bfloat16 [2, 128, 197, 384], P('branch', 'dp'), may hold values from -6 to 6
- live_counts: int32 [2, 16], P(None, 'dp'), may hold values from 1 to 8, as said below
- master: float32 [3257856], P(('branch', 'dp'))
- first_moment: float32 [3257856], P(('branch', 'dp')), may hold values from -0.0034179688 to 0.0034179688
- second_moment: float32 [3257856], P(('branch', 'dp')), may hold values from 3.0695034e-07 to 1.2278014e-06
Outputs:
- small_out: bfloat16 [2, 128, 145, 192], P('branch', 'dp')
- large_out: bfloat16 [2, 128, 197, 384], P('branch', 'dp')
- small_grad: bfloat16 [2, 128, 145, 192], P('branch', 'dp')
- large_grad: bfloat16 [2, 128, 197, 384], P('branch', 'dp')
- grad_norm: float32 [], replicated
- new_first: float32 [3257856], P(('branch', 'dp'))
- new_second: float32 [3257856], P(('branch', 'dp'))
- new_master: float32 [3257856], P(('branch', 'dp'))
- new_master16: bfloat16 [3257856], P(('branch', 'dp'))
Inputs may be any that keep to these rules, and one draw needn't show every extreme that they name: `live_counts`: 8 is reached in every draw.
All inputs are finite; a program needn't handle non-finite values.
Results may differ from a plain program's by a relative error of at most 0.014.
The roundings to bfloat16 on the way count: a program that leaves them out, or rounds other values in their place, can miss the bound.
Values may be sent and summed in bfloat16 or wider, within the bound.
No kernel may reach another device: no remote copies, remote signals or barrier semaphores. Data moves between devices by JAX's collectives and lax.ppermute only.
A program may use at most 192 MiB of HBM per device.

v0:
```python
import math

import jax
import jax.numpy as jnp
from jax import lax
from jax.sharding import PartitionSpec as P

DS = 192
DL = 384
MS = 768
ML = 1536
HEADS = 6


norm_eps = 1e-06
clip_norm = 1.0
beta_one = 0.5
beta_two = 0.5
adam_eps = 1e-08
rate = 0.05
decay = 0.05
bias_one = 1.0 - 0.5**5
bias_two = 1.0 - 0.5**5


def partner(value, axis, bit):
    return lax.ppermute(value, axis, [(i, i ^ 1 << bit) for i in range(lax.axis_size(axis))])


def layout():
    shapes = []
    for label, width, hidden in (("s", DS, MS), ("l", DL, ML)):
        shapes += [
            (label + "_ln1", (2, width)),
            (label + "_qkv_w", (width, 3 * width)),
            (label + "_qkv_b", (3 * width,)),
            (label + "_proj_w", (width, width)),
            (label + "_proj_b", (width,)),
            (label + "_ln2", (2, width)),
            (label + "_fc1_w", (width, hidden)),
            (label + "_fc1_b", (hidden,)),
            (label + "_fc2_w", (hidden, width)),
            (label + "_fc2_b", (width,)),
        ]
    for label, owner, other in (("s", DS, DL), ("l", DL, DS)):
        shapes += [
            (label + "_to_ln", (2, owner)),
            (label + "_to_w", (owner, other)),
            (label + "_to_b", (other,)),
            (label + "_ca_ln", (2, other)),
            (label + "_ca_q_w", (other, other)),
            (label + "_ca_q_b", (other,)),
            (label + "_ca_k_w", (other, other)),
            (label + "_ca_v_w", (other, other)),
            (label + "_ca_v_b", (other,)),
            (label + "_ca_o_w", (other, other)),
            (label + "_ca_o_b", (other,)),
            (label + "_back_ln", (2, other)),
            (label + "_back_w", (other, owner)),
            (label + "_back_b", (owner,)),
        ]
    return shapes


def unflatten(flat):
    params = {}
    offset = 0
    for label, shape in layout():
        count = math.prod(shape)
        params[label] = flat[offset : offset + count].reshape(shape)
        offset = offset + count
    return params


def narrow(value):
    return value.astype(jnp.bfloat16)


def widen(value):
    return value.astype(jnp.float32)


def norm_rows(value, pair):
    mean = jnp.mean(value, -1, keepdims=True)
    centred = value - mean
    variance = jnp.mean(centred * centred, -1, keepdims=True)
    return centred * lax.rsqrt(variance + norm_eps) * pair[0] + pair[1]


def gelu_exact(value):
    return jax.nn.gelu(value, approximate=False)


def product(left, right):
    return lax.dot_general(
        left, right, (((left.ndim - 1,), (0,)), ((), ())), preferred_element_type=jnp.float32
    )


def product_back(grad, right):
    return lax.dot_general(
        grad, right, (((grad.ndim - 1,), (1,)), ((), ())), preferred_element_type=jnp.float32
    )


def weight_grad(inputs, grad):
    rows_in = inputs.reshape(-1, inputs.shape[-1])
    rows_grad = grad.reshape(-1, grad.shape[-1])
    return lax.dot_general(
        rows_in, rows_grad, (((0,), (0,)), ((), ())), preferred_element_type=jnp.float32
    )


def bias_grad(grad):
    return jnp.sum(grad.reshape(-1, grad.shape[-1]), 0, dtype=jnp.float32)


def softmax_keep(scores):
    summit = jnp.max(scores, -1, keepdims=True)
    expwts = jnp.exp(scores - summit)
    totals = jnp.sum(expwts, -1, keepdims=True)
    return (expwts / totals, summit + jnp.log(totals))


def softmax_back(probs, probs_grad):
    return probs * (probs_grad - jnp.sum(probs_grad * probs, -1, keepdims=True))


def block_forward(tokens, params, label, heads):
    crops, length, width = tokens.shape
    size = width // heads
    scale = size ** (-0.5)
    normed, first_pull = jax.vjp(norm_rows, tokens, widen(params[label + "_ln1"]))
    normed_low = narrow(normed)
    mixed = narrow(product(normed_low, params[label + "_qkv_w"]) + widen(params[label + "_qkv_b"]))
    shaped = mixed.reshape(crops, length, 3, heads, size)
    query = shaped[:, :, 0]
    key = shaped[:, :, 1]
    value = shaped[:, :, 2]
    scores = jnp.einsum("bqhd,bkhd->bhqk", query, key, preferred_element_type=jnp.float32) * scale
    probs, summit = softmax_keep(scores)
    attended = narrow(
        jnp.einsum(
            "bhqk,bkhd->bqhd", narrow(probs), value, preferred_element_type=jnp.float32
        ).reshape(crops, length, width)
    )
    middle = (
        tokens + product(attended, params[label + "_proj_w"]) + widen(params[label + "_proj_b"])
    )
    normed_two, second_pull = jax.vjp(norm_rows, middle, widen(params[label + "_ln2"]))
    normed_two_low = narrow(normed_two)
    inner = product(normed_two_low, params[label + "_fc1_w"]) + widen(params[label + "_fc1_b"])
    activated, gelu_pull = jax.vjp(gelu_exact, inner)
    hidden = narrow(activated)
    output = middle + product(hidden, params[label + "_fc2_w"]) + widen(params[label + "_fc2_b"])
    kept = (
        first_pull,
        normed_low,
        query,
        key,
        value,
        summit,
        attended,
        second_pull,
        normed_two_low,
        gelu_pull,
        hidden,
    )
    return (output, kept)


def block_backward(grad_out, kept, params, label, heads, grads):
    (
        first_pull,
        normed_low,
        query,
        key,
        value,
        summit,
        attended,
        second_pull,
        normed_two_low,
        gelu_pull,
        hidden,
    ) = kept
    crops, length, width = grad_out.shape
    size = width // heads
    scale = size ** (-0.5)
    out_low = narrow(grad_out)
    grads[label + "_fc2_w"] = weight_grad(hidden, out_low)
    grads[label + "_fc2_b"] = bias_grad(out_low)
    inner_low = narrow(gelu_pull(product_back(out_low, params[label + "_fc2_w"]))[0])
    grads[label + "_fc1_w"] = weight_grad(normed_two_low, inner_low)
    grads[label + "_fc1_b"] = bias_grad(inner_low)
    middle_grad, second_grad = second_pull(product_back(inner_low, params[label + "_fc1_w"]))
    grads[label + "_ln2"] = second_grad
    middle_grad = middle_grad + grad_out
    middle_low = narrow(middle_grad)
    grads[label + "_proj_w"] = weight_grad(attended, middle_low)
    grads[label + "_proj_b"] = bias_grad(middle_low)
    attended_grad = narrow(product_back(middle_low, params[label + "_proj_w"])).reshape(
        crops, length, heads, size
    )
    scores = jnp.einsum("bqhd,bkhd->bhqk", query, key, preferred_element_type=jnp.float32) * scale
    probs = jnp.exp(scores - summit)
    probs_grad = jnp.einsum(
        "bqhd,bkhd->bhqk", attended_grad, value, preferred_element_type=jnp.float32
    )
    value_grad = narrow(
        jnp.einsum(
            "bhqk,bqhd->bkhd", narrow(probs), attended_grad, preferred_element_type=jnp.float32
        )
    )
    scores_grad = narrow(softmax_back(probs, probs_grad))
    query_grad = narrow(
        jnp.einsum("bhqk,bkhd->bqhd", scores_grad, key, preferred_element_type=jnp.float32) * scale
    )
    key_grad = narrow(
        jnp.einsum("bhqk,bqhd->bkhd", scores_grad, query, preferred_element_type=jnp.float32)
        * scale
    )
    mixed_grad = jnp.stack([query_grad, key_grad, value_grad], 2).reshape(crops, length, 3 * width)
    grads[label + "_qkv_w"] = weight_grad(normed_low, mixed_grad)
    grads[label + "_qkv_b"] = bias_grad(mixed_grad)
    tokens_grad, first_grad = first_pull(product_back(mixed_grad, params[label + "_qkv_w"]))
    grads[label + "_ln1"] = first_grad
    return tokens_grad + middle_grad


def carry_forward(value, params, prefix):
    normed, norm_pull = jax.vjp(norm_rows, value, widen(params[prefix + "_ln"]))
    activated, gelu_pull = jax.vjp(gelu_exact, normed)
    activated_low = narrow(activated)
    result = narrow(product(activated_low, params[prefix + "_w"]) + widen(params[prefix + "_b"]))
    return (result, (norm_pull, gelu_pull, activated_low))


def carry_backward(result_grad, kept, params, prefix, grads):
    norm_pull, gelu_pull, activated_low = kept
    grads[prefix + "_w"] = weight_grad(activated_low, result_grad)
    grads[prefix + "_b"] = bias_grad(result_grad)
    normed_grad = gelu_pull(product_back(result_grad, params[prefix + "_w"]))[0]
    value_grad, pair_grad = norm_pull(normed_grad)
    grads[prefix + "_ln"] = pair_grad
    return value_grad


def cross_forward(sent, patches, params, label, heads):
    crops, rows, width = patches.shape
    size = width // heads
    scale = size ** (-0.5)
    joined = jnp.concatenate([widen(sent)[:, None], patches], 1)
    normed, norm_pull = jax.vjp(norm_rows, joined, widen(params[label + "_ca_ln"]))
    normed_low = narrow(normed)
    query = narrow(
        product(normed_low[:, 0], params[label + "_ca_q_w"]) + widen(params[label + "_ca_q_b"])
    ).reshape(crops, heads, size)
    key = narrow(product(normed_low, params[label + "_ca_k_w"])).reshape(
        crops, rows + 1, heads, size
    )
    value = narrow(
        product(normed_low, params[label + "_ca_v_w"]) + widen(params[label + "_ca_v_b"])
    ).reshape(crops, rows + 1, heads, size)
    scores = jnp.einsum("bhd,bkhd->bhk", query, key, preferred_element_type=jnp.float32) * scale
    probs, summit = softmax_keep(scores)
    attended = narrow(
        jnp.einsum(
            "bhk,bkhd->bhd", narrow(probs), value, preferred_element_type=jnp.float32
        ).reshape(crops, width)
    )
    merged = (
        widen(sent)
        + product(attended, params[label + "_ca_o_w"])
        + widen(params[label + "_ca_o_b"])
    )
    return (merged, (norm_pull, normed_low, query, key, value, summit, attended))


def cross_backward(merged_grad, kept, params, label, grads):
    norm_pull, normed_low, query, key, value, summit, attended = kept
    crops, heads_here, size = query.shape
    rows = key.shape[1]
    width = heads_here * size
    scale = size ** (-0.5)
    merged_low = narrow(merged_grad)
    grads[label + "_ca_o_w"] = weight_grad(attended, merged_low)
    grads[label + "_ca_o_b"] = bias_grad(merged_low)
    attended_grad = narrow(product_back(merged_low, params[label + "_ca_o_w"])).reshape(
        crops, heads_here, size
    )
    scores = jnp.einsum("bhd,bkhd->bhk", query, key, preferred_element_type=jnp.float32) * scale
    probs = jnp.exp(scores - summit)
    probs_grad = jnp.einsum(
        "bhd,bkhd->bhk", attended_grad, value, preferred_element_type=jnp.float32
    )
    value_grad = narrow(
        jnp.einsum(
            "bhk,bhd->bkhd", narrow(probs), attended_grad, preferred_element_type=jnp.float32
        )
    ).reshape(crops, rows, width)
    scores_grad = narrow(softmax_back(probs, probs_grad))
    query_grad = narrow(
        jnp.einsum("bhk,bkhd->bhd", scores_grad, key, preferred_element_type=jnp.float32) * scale
    ).reshape(crops, width)
    key_grad = narrow(
        jnp.einsum("bhk,bhd->bkhd", scores_grad, query, preferred_element_type=jnp.float32) * scale
    ).reshape(crops, rows, width)
    grads[label + "_ca_q_w"] = weight_grad(normed_low[:, 0], query_grad)
    grads[label + "_ca_q_b"] = bias_grad(query_grad)
    grads[label + "_ca_k_w"] = weight_grad(normed_low, key_grad)
    grads[label + "_ca_v_w"] = weight_grad(normed_low, value_grad)
    grads[label + "_ca_v_b"] = bias_grad(value_grad)
    normed_grad = product_back(key_grad, params[label + "_ca_k_w"]) + product_back(
        value_grad, params[label + "_ca_v_w"]
    )
    head_row = normed_grad[:, 0] + product_back(query_grad, params[label + "_ca_q_w"])
    normed_grad = jnp.concatenate([head_row[:, None], normed_grad[:, 1:]], 1)
    joined_grad, pair_grad = norm_pull(normed_grad)
    grads[label + "_ca_ln"] = pair_grad
    return (joined_grad[:, 0] + merged_grad, joined_grad[:, 1:])


def shards(
    small_tokens,
    large_tokens,
    small_cot,
    large_cot,
    live_counts,
    master,
    first_moment,
    second_moment,
):
    flat_weights = lax.all_gather(narrow(master), ("branch", "dp"), axis=0, tiled=True)
    params = unflatten(flat_weights)
    small = widen(small_tokens[0])
    large = widen(large_tokens[0])
    small_block, small_kept = block_forward(small, params, "s", HEADS)
    large_block, large_kept = block_forward(large, params, "l", HEADS)
    sent_small, small_to = carry_forward(small_block[:, 0], params, "s_to")
    sent_large, large_to = carry_forward(large_block[:, 0], params, "l_to")
    got_small, got_large = partner((sent_small, sent_large), "branch", 0)
    merged_small, small_cross = cross_forward(got_small, large_block[:, 1:], params, "s", HEADS)
    merged_large, large_cross = cross_forward(got_large, small_block[:, 1:], params, "l", HEADS)
    back_small, small_revert = carry_forward(merged_small, params, "s_back")
    back_large, large_revert = carry_forward(merged_large, params, "l_back")
    home_small, home_large = partner((back_small, back_large), "branch", 0)
    small_final = jnp.concatenate([widen(home_small)[:, None], small_block[:, 1:]], 1)
    large_final = jnp.concatenate([widen(home_large)[:, None], large_block[:, 1:]], 1)
    half = lax.axis_index("branch")
    counts = live_counts[:, 0]
    own_count = lax.dynamic_index_in_dim(counts, half, 0, False)
    far_count = lax.dynamic_index_in_dim(counts, 1 - half, 0, False)
    slots = jnp.arange(small.shape[0], dtype=jnp.int32)
    small_live = (slots < own_count).astype(jnp.float32)[:, None, None]
    large_live = (slots < far_count).astype(jnp.float32)[:, None, None]
    small_seed = widen(small_cot[0]) * small_live
    large_seed = widen(large_cot[0]) * large_live
    grads = {}
    ret_small, ret_large = partner(
        (narrow(small_seed[:, 0]), narrow(large_seed[:, 0])), "branch", 0
    )
    merged_small_grad = carry_backward(ret_small, small_revert, params, "s_back", grads)
    merged_large_grad = carry_backward(ret_large, large_revert, params, "l_back", grads)
    sent_small_grad, large_patch_grad = cross_backward(
        merged_small_grad, small_cross, params, "s", grads
    )
    sent_large_grad, small_patch_grad = cross_backward(
        merged_large_grad, large_cross, params, "l", grads
    )
    own_small, own_large = partner((narrow(sent_small_grad), narrow(sent_large_grad)), "branch", 0)
    small_head_grad = carry_backward(own_small, small_to, params, "s_to", grads)
    large_head_grad = carry_backward(own_large, large_to, params, "l_to", grads)
    small_block_grad = jnp.concatenate(
        [small_head_grad[:, None], small_seed[:, 1:] + small_patch_grad], 1
    )
    large_block_grad = jnp.concatenate(
        [large_head_grad[:, None], large_seed[:, 1:] + large_patch_grad], 1
    )
    small_input_grad = block_backward(small_block_grad, small_kept, params, "s", HEADS, grads)
    large_input_grad = block_backward(large_block_grad, large_kept, params, "l", HEADS, grads)
    flat_grad = jnp.concatenate([grads[label].reshape(-1) for label, shape in layout()])
    shard = master.shape[0]
    summed = lax.psum(flat_grad, ("branch", "dp"))
    grad_norm = jnp.sqrt(jnp.sum(summed * summed))
    own_grad = lax.dynamic_slice_in_dim(summed, lax.axis_index(("branch", "dp")) * shard, shard)
    clipped = own_grad * jnp.minimum(1.0, clip_norm / grad_norm)
    new_first = beta_one * first_moment + (1.0 - beta_one) * clipped
    new_second = beta_two * second_moment + (1.0 - beta_two) * clipped * clipped
    new_master = master - rate * (
        new_first / bias_one / (jnp.sqrt(new_second / bias_two) + adam_eps) + decay * master
    )
    return (
        narrow(small_final)[None],
        narrow(large_final)[None],
        narrow(small_input_grad)[None],
        narrow(large_input_grad)[None],
        grad_norm,
        new_first,
        new_second,
        new_master,
        narrow(new_master),
    )


def solution(mesh):
    return jax.shard_map(
        shards,
        mesh=mesh,
        in_specs=(
            P("branch", "dp", None, None),
            P("branch", "dp", None, None),
            P("branch", "dp", None, None),
            P("branch", "dp", None, None),
            P(None, "dp"),
            P(("branch", "dp")),
            P(("branch", "dp")),
            P(("branch", "dp")),
        ),
        out_specs=(
            P("branch", "dp", None, None),
            P("branch", "dp", None, None),
            P("branch", "dp", None, None),
            P("branch", "dp", None, None),
            P(),
            P(("branch", "dp")),
            P(("branch", "dp")),
            P(("branch", "dp")),
            P(("branch", "dp")),
        ),
        check_vma=False,
    )
```

profile of v0, /device:TPU:0, one launch (start us, length us, event | category | flops | bytes accessed | tf_op | source)
XLA Modules:
  0.0 1070.7 jit_solution(13779607403160121353)
XLA Ops:
  11.3 4.4 dynamic-update-slice
  25.7 151.4 %all-reduce.26.cloned.1.call-done = bf16[3257856]{0:T(1024)(128)(2,1)} async-done(((bf16[3257856]{0:T(1024)(128)(2,1)}), bf16[3257856]{0:T(1024)(128)(2,1)}) %all-reduce.26.cloned.1.call-update) | async-done | bytes 6515728
  197.7 3.9 fusion.71
  206.0 5.7 add_convert_fusion.1
  211.7 6.8 copy.78
  218.5 3.4 multiply_reduce_fusion.2
  225.6 5.1 fusion.54
  238.7 3.7 fusion.417
  245.5 3.5 fusion.416
  261.9 9.4 multiply_convert_fusion.3
  281.3 5.3 fusion.40
  286.7 23.8 %multiply_convert_fusion.1 = (bf16[8,197,1536]{2,1,0:T(8,128)(2,1)S(1)}, f32[8,197,1536]{2,1,0:T(8,128)}) fusion(f32[8,197,1536]{2,1,0:T(8,128)S(1)} %get-tuple-element.196, f32[1536]{0:T(1024)S(1)} %slice_convert_fusion.2, u8[197,1536]{1,0:T(8,128)(4,1)S(1)} %get-tuple-element.28, u8[197,1536]{1,0:T(8,128)(4,1)S(1)} %get-tuple-element.27), kind=kLoop, calls=%fused_computation.15 | loop fusion | flops 171872256 | bytes 24818688 | tf_op jit(solution)/shard_map/convert_element_type | solution.py:76
  413.6 3.4 add_convert_fusion.4
  419.6 3.4 convolution_convert_fusion.1
  458.6 4.0 multiply_reduce_fusion.5
  472.6 4.6 convolution_bitcast_fusion
  477.3 10.0 convert_reduce_fusion
  487.4 6.8 fusion.36
  500.3 3.3 fusion.406
  509.9 5.7 fusion.64
  515.6 8.5 multiply_reduce_fusion.1
  524.1 11.4 %multiply_convert_fusion = bf16[8,6,197,197]{2,3,1,0:T(8,128)(2,1)} fusion(f32[8,6,197,197]{2,3,1,0:T(8,128)} %get-tuple-element.210, f32[8,6,197,197]{2,3,1,0:T(8,128)} %copy-done, f32[8,6,197]{2,1,0:T(8,128)S(1)} %get-tuple-element.209, f32[8,6,197]{2,1,0:T(8,128)S(1)} %copy-done.85), kind=kLoop, calls=%fused_computation.11 | loop fusion | flops 9314160 | bytes 18703968 | tf_op jit(solution)/shard_map/convert_element_type | solution.py:76
  535.6 4.7 fusion.68
  544.5 5.4 copy.132
  567.0 9.1 reshape_reshape.23
  576.2 5.3 fusion.434
  582.6 3.9 fusion.44
  632.3 4.8 fusion.78
  670.4 146.3 %concatenate.63 = f32[3257856]{0:T(1024)} concatenate(f32[384]{0:T(512)S(1)} %reshape.1484, f32[110592]{0:T(1024)} %reshape.1485, f32[576]{0:T(1024)S(1)} %reduce_sum.1040, f32[36864]{0:T(1024)} %reshape.1486, f32[192]{0:T(256)S(1)} %copy-done.240, f32[384]{0:T(512)S(1)} %reshape.1487, f32[147456]{0:T(1024)} %reshape.1488, f32[768]{0:T(1024)S(1)} %copy-done.239, ...), dimensions={0} | concatenate | bytes 26062848 | tf_op jit(solution)/shard_map/concatenate | solution.py:381
  823.9 5.6 fusion.94
  832.8 219.1 %all-reduce.24.cloned.1.call-done = f32[3257856]{0:T(1024)} async-done(((f32[3257856]{0:T(1024)}), f32[3257856]{0:T(1024)}) %all-reduce.24.cloned.1.call-update) | async-done | bytes 13031440 | tf_op jit(solution)/shard_map/psum | solution.py:383
  1051.9 7.3 multiply_reduce_fusion
  (925 shorter events, 351.9 us)
Async XLA Ops:
  7.2 169.9 %all-reduce.26.cloned.1.call-start = ((), (), s32[]{:S(2)}) async-start(), calls=%async_computation.1 | async-start | bytes 13033472
  15.7 1036.2 %all-reduce.24.cloned.1.call-start = ((), (), s32[]{:S(2)}) async-start(), calls=%async_computation | async-start | bytes 26066944 | tf_op jit(solution)/shard_map/psum | solution.py:383
  17.8 6.7 collective-permute-start.4
  21.2 3.9 collective-permute-start.6
  22.1 165.0 %copy-start.114 = (f32[8,145]{1,0:T(8,128)}, f32[8,145]{1,0:T(8,128)S(1)}, u32[]{:S(2)}) copy-start(f32[8,145]{1,0:T(8,128)S(1)} %broadcast_multiply_fusion.5) | copy-start | bytes 13924
  22.7 155.2 %copy-start.139 = (f32[8,145]{1,0:T(8,128)}, f32[8,145]{1,0:T(8,128)S(1)}, u32[]{:S(2)}) copy-start(f32[8,145]{1,0:T(8,128)S(1)} %fusion.83) | copy-start | bytes 13924
  23.0 158.6 %copy-start.36 = (f32[8,197]{0,1:T(8,128)}, f32[8,197]{0,1:T(8,128)S(1)}, u32[]{:S(2)}) copy-start(f32[8,197]{0,1:T(8,128)S(1)} %broadcast_multiply_fusion.2) | copy-start | bytes 18916
  24.5 157.2 %copy-start.53 = (f32[8,197]{0,1:T(8,128)}, f32[8,197]{0,1:T(8,128)S(1)}, u32[]{:S(2)}) copy-start(f32[8,197]{0,1:T(8,128)S(1)} %fusion.132) | copy-start | bytes 18916
  24.5 162.6 %copy-start.126 = (f32[8,145]{1,0:T(8,128)}, f32[8,145]{1,0:T(8,128)S(1)}, u32[]{:S(2)}) copy-start(f32[8,145]{1,0:T(8,128)S(1)} %fusion.222) | copy-start | bytes 13924
  24.5 157.2 %copy-start.173 = (bf16[8,192]{1,0:T(8,128)(2,1)}, bf16[8,192]{1,0:T(8,128)(2,1)S(1)}, u32[]{:S(2)}) copy-start(bf16[8,192]{1,0:T(8,128)(2,1)S(1)} %collective-permute-done.4) | copy-start | bytes 9220
  25.1 155.0 %copy-start.167 = (bf16[8,384]{1,0:T(8,128)(2,1)}, bf16[8,384]{1,0:T(8,128)(2,1)S(1)}, u32[]{:S(2)}) copy-start(bf16[8,384]{1,0:T(8,128)(2,1)S(1)} %collective-permute-done.6) | copy-start | bytes 18436
  177.9 84.0 %copy-start.171 = (f32[768]{0:T(1024)}, f32[768]{0:T(1024)S(1)}, u32[]{:S(2)}) copy-start(f32[768]{0:T(1024)S(1)} %get-tuple-element.133) | copy-start | bytes 9220
  185.2 74.8 %copy-start.187 = (f32[192]{0:T(256)}, f32[192]{0:T(256)S(1)}, u32[]{:S(2)}) copy-start(f32[192]{0:T(256)S(1)} %get-tuple-element.181) | copy-start | bytes 2308
  185.2 74.8 %copy-start.194 = (f32[192]{0:T(256)}, f32[192]{0:T(256)S(1)}, u32[]{:S(2)}) copy-start(f32[192]{0:T(256)S(1)} %get-tuple-element.182) | copy-start | bytes 2308
  232.6 82.6 %copy-start.179 = (f32[192]{0:T(256)}, f32[192]{0:T(256)S(1)}, u32[]{:S(2)}) copy-start(f32[192]{0:T(256)S(1)} %get-tuple-element.179) | copy-start | bytes 2308
  272.6 43.6 %copy-start.30 = (f32[8,145,192]{2,1,0:T(8,128)}, f32[8,145,192]{2,1,0:T(8,128)S(1)}, u32[]{:S(2)}) copy-start(f32[8,145,192]{2,1,0:T(8,128)S(1)} %fusion.69) | copy-start | bytes 2672644
  272.7 42.5 %copy-start.118 = (f32[8,1,192]{2,1,0:T(1,128)}, f32[8,1,192]{2,1,0:T(1,128)S(1)}, u32[]{:S(2)}) copy-start(f32[8,1,192]{2,1,0:T(1,128)S(1)} %get-tuple-element.148) | copy-start | bytes 18436
  272.7 42.5 %copy-start.206 = (f32[8]{0:T(128)}, f32[8]{0:T(128)S(1)}, u32[]{:S(2)}) copy-start(f32[8]{0:T(128)S(1)} %broadcast_multiply_fusion.9) | copy-start | bytes 100
  272.9 42.3 %copy-start.229 = (f32[8]{0:T(128)}, f32[8]{0:T(128)S(1)}, u32[]{:S(2)}) copy-start(f32[8]{0:T(128)S(1)} %fusion.315) | copy-start | bytes 100
  278.5 34.9 %copy-start.2 = (f32[8,197,384]{2,0,1:T(8,128)}, f32[8,197,384]{2,0,1:T(8,128)S(1)}, u32[]{:S(2)}) copy-start(f32[8,197,384]{2,0,1:T(8,128)S(1)} %get-tuple-element.195) | copy-start | bytes 7262212
  279.2 35.1 %copy-start.160 = (f32[384]{0:T(512)}, f32[384]{0:T(512)S(1)}, u32[]{:S(2)}) copy-start(f32[384]{0:T(512)S(1)} %get-tuple-element.165) | copy-start | bytes 4612
  279.2 35.1 %copy-start.210 = (f32[384]{0:T(512)}, f32[384]{0:T(512)S(1)}, u32[]{:S(2)}) copy-start(f32[384]{0:T(512)S(1)} %get-tuple-element.166) | copy-start | bytes 4612
  315.2 19.4 %collective-permute-start.2 = (bf16[8,192]{1,0:T(8,128)(2,1)S(1)}, bf16[8,192]{1,0:T(8,128)(2,1)S(1)}, u32[]{:S(2)}, u32[]{:S(2)}) collective-permute-start(bf16[8,192]{1,0:T(8,128)(2,1)S(1)} %fusion.107), channel_id=1, source_target_pairs={{0,16},{16,0},{1,17},{17,1},{2,18},{18,2},{3,19},{19,3},{4,20},{20... | collective-permute-start | bytes 9224 | tf_op jit(solution)/shard_map/ppermute | solution.py:27
  334.1 75.7 %collective-permute-start = (bf16[8,384]{1,0:T(8,128)(2,1)}, bf16[8,384]{1,0:T(8,128)(2,1)}, u32[]{:S(2)}, u32[]{:S(2)}) collective-permute-start(bf16[8,384]{1,0:T(8,128)(2,1)} %fusion.102), channel_id=1, source_target_pairs={{0,16},{16,0},{1,17},{17,1},{2,18},{18,2},{3,19},{19,3},{4,20},{20... | collective-permute-start | bytes 18440 | tf_op jit(solution)/shard_map/ppermute | solution.py:27
  409.6 58.5 %collective-permute-start.7 = (bf16[8,192]{1,0:T(8,128)(2,1)S(1)}, bf16[8,192]{1,0:T(8,128)(2,1)S(1)}, u32[]{:S(2)}, u32[]{:S(2)}) collective-permute-start(bf16[8,192]{1,0:T(8,128)(2,1)S(1)} %fusion.204), channel_id=1, source_target_pairs={{0,16},{16,0},{1,17},{17,1},{2,18},{18,2},{3,19},{19,3},{4,20},{20... | collective-permute-start | bytes 9224 | tf_op jit(solution)/shard_map/ppermute | solution.py:27
  464.5 39.1 %copy-start.10 = (f32[8,196,384]{2,0,1:T(8,128)}, f32[8,196,384]{2,0,1:T(8,128)S(1)}, u32[]{:S(2)}) copy-start(f32[8,196,384]{2,0,1:T(8,128)S(1)} %slice_add_fusion) | copy-start | bytes 7225348
  566.6 47.3 %collective-permute-start.5 = (bf16[8,384]{1,0:T(8,128)(2,1)S(1)}, bf16[8,384]{1,0:T(8,128)(2,1)S(1)}, u32[]{:S(2)}, u32[]{:S(2)}) collective-permute-start(bf16[8,384]{1,0:T(8,128)(2,1)S(1)} %copy-done.225), channel_id=1, source_target_pairs={{0,16},{16,0},{1,17},{17,1},{2,18},{18,2},{3,19},{19,3},{4,20},{20... | collective-permute-start | bytes 18440 | tf_op jit(solution)/shard_map/ppermute | solution.py:27
  821.3 9.4 collective-permute-start.3
  822.6 7.0 collective-permute-start.1
  832.8 227.2 %copy-start.62 = (f32[101808]{0:T(1024)S(1)}, f32[101808]{0:T(1024)}, u32[]{:S(2)}) copy-start(f32[101808]{0:T(1024)} %param.13) | copy-start | bytes 1221700
  832.8 227.2 %copy-start.106 = (f32[101808]{0:T(1024)S(1)}, f32[101808]{0:T(1024)}, u32[]{:S(2)}) copy-start(f32[101808]{0:T(1024)} %param.15) | copy-start | bytes 1221700
  832.8 227.2 %copy-start.107 = (f32[101808]{0:T(1024)S(1)}, f32[101808]{0:T(1024)}, u32[]{:S(2)}) copy-start(f32[101808]{0:T(1024)} %param.14) | copy-start | bytes 1221700
  (252 other events, 1160.8 us)
Sparse Core Ops, SparseCore 0:
  15.8 161.2 all-reduce.25
  816.9 235.0 all-reduce.23
where the time goes:
time: 1090 us; the launch traced here: 1070 us
  waiting for transfers between devices  371 us (34%)
  local copies, waits for them, and re-layouts  346 us (32%)
  matrix products  174 us (16%)
  other arithmetic  158 us (14%)
  between operations  19.7 us (2%)
    psum x1, waiting for transfers between devices, shards(): summed = lax.psum(flat_grad, ('branch', 'dp'))  219 us
    unnamed x3, waiting for transfers between devices  151 us
    concatenate x1, local copies, waits for them, and re-layouts, shards(): jnp.concatenate([grads[label].reshape(-1) for label, shape in layout()])  146 us
    convert_element_type x18, other arithmetic, narrow(): return value.astype(jnp.bfloat16)  65.3 us
    convert_element_type x20, local copies, waits for them, and re-layouts, narrow(): return value.astype(jnp.bfloat16)  41.9 us
    dot_general x20, matrix products, product_back(): lax.dot_general(grad, right, (((grad.ndim - 1,), (1,)), ((), ())), prefer...  40.9 us
    dot_general x20, matrix products, weight_grad(): lax.dot_general(rows_in, rows_grad, (((0,), (0,)), ((), ())), preferred_e...  39.6 us
    dot_general x20, matrix products, product(): lax.dot_general(left, right, (((left.ndim - 1,), (0,)), ((), ())), prefer...  38 us
  transfers between devices with their start and end apart: 10, of which 2 were waited for; matrix products, arithmetic and copies ran while one was open for 20% of the time, Pallas kernels for 0%

commit v1 on v0

v1 whole, which is shorter than its diff:
```python
import functools
import math

import jax
import jax.numpy as jnp
import numpy as np
from jax import lax
from jax.experimental import pallas as pl
from jax.experimental.pallas import tpu as pltpu
from jax.sharding import PartitionSpec as P

DS = 192
DL = 384
MS = 768
ML = 1536
HEADS = 6

norm_eps = 1e-06
clip_norm = 1.0
beta_one = 0.5
beta_two = 0.5
adam_eps = 1e-08
rate = 0.05
decay = 0.05
bias_one = 1.0 - 0.5**5
bias_two = 1.0 - 0.5**5

f32 = jnp.float32
bf16 = jnp.bfloat16
LANES = 128


def layout():
    shapes = []
    for label, width, hidden in (("s", DS, MS), ("l", DL, ML)):
        shapes += [
            (label + "_ln1", (2, width)),
            (label + "_qkv_w", (width, 3 * width)),
            (label + "_qkv_b", (3 * width,)),
            (label + "_proj_w", (width, width)),
            (label + "_proj_b", (width,)),
            (label + "_ln2", (2, width)),
            (label + "_fc1_w", (width, hidden)),
            (label + "_fc1_b", (hidden,)),
            (label + "_fc2_w", (hidden, width)),
            (label + "_fc2_b", (width,)),
        ]
    for label, owner, other in (("s", DS, DL), ("l", DL, DS)):
        shapes += [
            (label + "_to_ln", (2, owner)),
            (label + "_to_w", (owner, other)),
            (label + "_to_b", (other,)),
            (label + "_ca_ln", (2, other)),
            (label + "_ca_q_w", (other, other)),
            (label + "_ca_q_b", (other,)),
            (label + "_ca_k_w", (other, other)),
            (label + "_ca_v_w", (other, other)),
            (label + "_ca_v_b", (other,)),
            (label + "_ca_o_w", (other, other)),
            (label + "_ca_o_b", (other,)),
            (label + "_back_ln", (2, other)),
            (label + "_back_w", (other, owner)),
            (label + "_back_b", (owner,)),
        ]
    return shapes


def round_up(value, unit):
    return -(-value // unit) * unit


def grid_plan(shards):
    names = []
    regions = []
    offset = 0
    for label, shape in layout():
        count = math.prod(shape)
        phase = offset % LANES
        if not regions or regions[-1][2] != phase:
            regions.append([offset, offset, phase])
        names.append((label, shape, offset, len(regions) - 1))
        offset += count
        regions[-1][1] = offset
    total = offset
    starts = []
    row = 0
    for first, last, phase in regions:
        starts.append(row)
        row += -(-(last - first) // LANES)
    rows = row
    places = {}
    for label, shape, place, region in names:
        places[label] = (starts[region] + (place - regions[region][0]) // LANES, shape)
    size = total // shards
    bases = []
    pieces = []
    for device in range(shards):
        low, high = device * size, (device + 1) * size
        own = []
        base = None
        for (first, last, phase), start in zip(regions, starts):
            left, right = max(low, first), min(high, last)
            if left >= right:
                continue
            if base is None:
                base = (start + (left - first) // LANES) // 16 * 16
            delta = start * LANES - first + low - base * LANES
            own.append((left - low, right - low, delta))
        bases.append(base)
        pieces.append(own)
    most = max(len(own) for own in pieces)
    table = np.zeros((shards, most * 3), np.int32)
    need = 0
    for device, own in enumerate(pieces):
        for number, (left, right, delta) in enumerate(own):
            table[device, 3 * number : 3 * number + 3] = (left, right, delta)
            need = max(need, right + delta)
    span = round_up(-(-need // LANES), 16)
    overlap = 16
    for device in range(1, shards):
        overlap = max(overlap, bases[device - 1] + span - bases[device])
    return dict(
        places=places,
        rows=rows,
        size=size,
        bases=bases,
        table=table,
        most=most,
        span=span,
        overlap=overlap,
        height=round_up(max(bases) + span + overlap, 16),
        shard_rows=round_up(-(-size // LANES), 16),
    )


def mm(left, right):
    return lax.dot_general(left, right, (((1,), (0,)), ((), ())), preferred_element_type=f32)


def mm_t(left, right):
    return lax.dot_general(left, right, (((1,), (1,)), ((), ())), preferred_element_type=f32)


def t_mm(left, right):
    return lax.dot_general(left, right, (((0,), (0,)), ((), ())), preferred_element_type=f32)


def vmem_spec(shape, index):
    return pl.BlockSpec(shape, index)


def whole(shape):
    rank = len(shape)
    return pl.BlockSpec(shape, lambda *_: (0,) * rank, pipeline_mode=pl.Buffered(1))


def estimate(flops, moved):
    return pl.CostEstimate(flops=int(flops), bytes_accessed=int(moved), transcendentals=0)


def shift_rows(ref, amount, rows, margin):
    down = amount // LANES
    across = amount - down * LANES
    here = ref[pl.ds(margin - down, rows), :]
    above = ref[pl.ds(margin - down - 1, rows), :]
    here = pltpu.roll(here, across, 1)
    above = pltpu.roll(above, across, 1)
    lane = lax.broadcasted_iota(jnp.int32, here.shape, 1)
    return jnp.where(lane < across, above, here)


def align_kernel(most, rows, span, margin, table_ref, shard_ref, out_ref, padded):
    padded[...] = jnp.zeros_like(padded)
    padded[margin : margin + rows, :] = shard_ref[...]
    place = lax.broadcasted_iota(jnp.int32, (span, LANES), 0) * LANES
    place = place + lax.broadcasted_iota(jnp.int32, (span, LANES), 1)
    total = jnp.zeros((span, LANES), f32)
    for number in range(most):
        left = table_ref[3 * number]
        right = table_ref[3 * number + 1]
        delta = table_ref[3 * number + 2]
        moved = shift_rows(padded, delta, span, margin)
        total = jnp.where((place >= left + delta) & (place < right + delta), moved, total)
    out_ref[...] = total.astype(bf16)


def unalign_kernel(most, rows, span, margin, table_ref, grid_ref, out_ref, norm_ref, padded):
    padded[...] = jnp.zeros_like(padded)
    padded[0:span, :] = grid_ref[...]
    place = lax.broadcasted_iota(jnp.int32, (rows, LANES), 0) * LANES
    place = place + lax.broadcasted_iota(jnp.int32, (rows, LANES), 1)
    total = jnp.zeros((rows, LANES), f32)
    lane = lax.broadcasted_iota(jnp.int32, (rows, LANES), 1)
    for number in range(most):
        left = table_ref[3 * number]
        right = table_ref[3 * number + 1]
        delta = table_ref[3 * number + 2]
        down = delta // LANES
        across = delta - down * LANES
        back = lax.rem(LANES - across, LANES)
        here = pltpu.roll(padded[pl.ds(down, rows), :], back, 1)
        below = pltpu.roll(padded[pl.ds(down + 1, rows), :], back, 1)
        moved = jnp.where(lane < LANES - across, here, below)
        total = jnp.where((place >= left) & (place < right), moved, total)
    out_ref[...] = total
    norm_ref[...] = jnp.broadcast_to(jnp.sum(total * total).reshape(1, 1), (8, LANES))


def align(shard, table, plan):
    rows, span, most = plan["shard_rows"], plan["span"], plan["most"]
    margin = 8 + round_up(int(plan["table"].max(initial=0, where=pick_delta(plan))) // LANES + 1, 8)
    tall = margin + max(rows, span) + 8
    return pl.pallas_call(
        functools.partial(align_kernel, most, rows, span, margin),
        out_shape=jax.ShapeDtypeStruct((span, LANES), bf16),
        in_specs=[
            pl.BlockSpec(memory_space=pltpu.SMEM),
            pl.BlockSpec(memory_space=pltpu.VMEM),
        ],
        out_specs=pl.BlockSpec(memory_space=pltpu.VMEM),
        scratch_shapes=[pltpu.VMEM((tall, LANES), f32)],
        name="align",
    )(table, shard)


def unalign(grid, table, plan):
    rows, span, most = plan["shard_rows"], plan["span"], plan["most"]
    margin = 16 + round_up(int(plan["table"].max(initial=0, where=pick_delta(plan))) // LANES + 1, 8)
    tall = max(rows, span) + margin
    return pl.pallas_call(
        functools.partial(unalign_kernel, most, rows, span, margin),
        out_shape=(
            jax.ShapeDtypeStruct((rows, LANES), f32),
            jax.ShapeDtypeStruct((8, LANES), f32),
        ),
        in_specs=[
            pl.BlockSpec(memory_space=pltpu.SMEM),
            pl.BlockSpec(memory_space=pltpu.VMEM),
        ],
        out_specs=(
            pl.BlockSpec(memory_space=pltpu.VMEM),
            pl.BlockSpec(memory_space=pltpu.VMEM),
        ),
        scratch_shapes=[pltpu.VMEM((tall, LANES), f32)],
        name="unalign",
    )(table, grid)


def pick_delta(plan):
    mask = np.zeros(plan["table"].shape, bool)
    mask[:, 2::3] = True
    return mask


def two_dim(shape):
    return shape if len(shape) == 2 else (1, shape[0])


def is_matrix(label):
    return label[-2:] == "_w"


def strided(start, count, step):
    return pl.ds(start, count) if step == 1 or count == 1 else pl.ds(start, count, stride=step)


def half_swap(value):
    return pltpu.roll(value, LANES // 2, 1)


def read_param(flat, row, shape, out_ref, pair_ref):
    depth, width = two_dim(shape)
    dtype = out_ref.dtype
    if width % LANES == 0:
        step = width // LANES
        for col in range(step):
            out_ref[:, col * LANES : (col + 1) * LANES] = flat[
                strided(row + col, depth, step), :
            ].astype(dtype)
        return
    half = LANES // 2
    lead = width // LANES
    if depth == 1:
        for col in range(lead):
            out_ref[:, col * LANES : (col + 1) * LANES] = flat[row + col : row + col + 1, :].astype(
                dtype
            )
        out_ref[:, lead * LANES :] = flat[row + lead : row + lead + 1, 0:half].astype(dtype)
        return
    step = 2 * width // LANES
    pairs = depth // 2
    lane = lax.broadcasted_iota(jnp.int32, (pairs, LANES), 1)
    blocks = [flat[strided(row + col, pairs, step), :] for col in range(step)]
    turned = [half_swap(block) for block in blocks[lead:]]
    for col in range(lead):
        pair_ref[col, strided(0, pairs, 2), :] = blocks[col]
        pair_ref[col, strided(1, pairs, 2), :] = jnp.where(lane < half, turned[col], turned[col + 1])
    pair_ref[lead, strided(0, pairs, 2), :] = blocks[lead]
    pair_ref[lead, strided(1, pairs, 2), :] = turned[lead]
    for col in range(lead):
        out_ref[:, col * LANES : (col + 1) * LANES] = pair_ref[col, 0:depth, :].astype(dtype)
    out_ref[:, lead * LANES :] = pair_ref[lead, 0:depth, 0:half].astype(dtype)


def write_param(flat, row, shape, in_ref, pair_ref):
    depth, width = two_dim(shape)
    if width % LANES == 0:
        step = width // LANES
        for col in range(step):
            flat[strided(row + col, depth, step), :] = in_ref[:, col * LANES : (col + 1) * LANES]
        return
    half = LANES // 2
    lead = width // LANES
    if depth == 1:
        for col in range(lead):
            flat[row + col : row + col + 1, :] = in_ref[:, col * LANES : (col + 1) * LANES]
        tail = jnp.concatenate([in_ref[:, lead * LANES :], jnp.zeros((1, half), f32)], 1)
        flat[row + lead : row + lead + 1, :] = tail
        return
    step = 2 * width // LANES
    pairs = depth // 2
    lane = lax.broadcasted_iota(jnp.int32, (pairs, LANES), 1)
    for col in range(lead):
        pair_ref[col, 0:depth, :] = in_ref[:, col * LANES : (col + 1) * LANES]
    pair_ref[lead, 0:depth, 0:half] = in_ref[:, lead * LANES :]
    even = [pair_ref[col, strided(0, pairs, 2), :] for col in range(lead + 1)]
    odd = [half_swap(pair_ref[col, strided(1, pairs, 2), :]) for col in range(lead + 1)]
    for col in range(lead):
        flat[strided(row + col, pairs, step), :] = even[col]
    flat[strided(row + lead, pairs, step), :] = jnp.where(lane < half, even[lead], odd[0])
    for col in range(lead):
        flat[strided(row + lead + 1 + col, pairs, step), :] = jnp.where(
            lane < half, odd[col], odd[col + 1]
        )


def unflatten_kernel(plan, shards, base_ref, grid_ref, *refs):
    outs, (flat, pair_ref) = refs[:-2], refs[-2:]
    span, overlap = plan["span"], plan["overlap"]
    flat[0:overlap, :] = jnp.zeros((overlap, LANES), f32)

    def place(device, carry):
        base = pl.multiple_of(base_ref[device], 16)
        head = flat[pl.ds(base, overlap), :]
        flat[pl.ds(base, span), :] = grid_ref[device].astype(f32)
        flat[pl.ds(base, overlap), :] += head
        flat[pl.ds(base + span, overlap), :] = jnp.zeros((overlap, LANES), f32)
        return carry

    lax.fori_loop(0, shards, place, 0)
    for (label, shape), out_ref in zip(layout(), outs):
        read_param(flat, plan["places"][label][0], shape, out_ref, pair_ref)


def unflatten(grid, plan, shards):
    outs = []
    for label, shape in layout():
        outs.append(jax.ShapeDtypeStruct(two_dim(shape), bf16 if is_matrix(label) else f32))
    vmem = pl.BlockSpec(memory_space=pltpu.VMEM)
    values = pl.pallas_call(
        functools.partial(unflatten_kernel, plan, shards),
        out_shape=outs,
        in_specs=[pl.BlockSpec(memory_space=pltpu.SMEM), vmem],
        out_specs=[vmem] * len(outs),
        scratch_shapes=[
            pltpu.VMEM((plan["height"], LANES), f32),
            pltpu.VMEM((5, MS, LANES), f32),
        ],
        name="unflatten",
    )(jnp.asarray(plan["bases"], jnp.int32), grid)
    return {label: value for (label, shape), value in zip(layout(), values)}


def flatten_kernel(plan, shards, base_ref, *refs):
    count = len(layout())
    grads, out_ref, flat, pair_ref = refs[:count], refs[count], refs[count + 1], refs[count + 2]
    span, rows = plan["span"], plan["rows"]
    tail = rows // 8 * 8
    flat[tail:, :] = jnp.zeros((plan["height"] - tail, LANES), f32)
    for (label, shape), ref in zip(layout(), grads):
        write_param(flat, plan["places"][label][0], shape, ref, pair_ref)

    def place(device, carry):
        base = pl.multiple_of(base_ref[device], 16)
        out_ref[device] = flat[pl.ds(base, span), :].astype(bf16)
        return carry

    lax.fori_loop(0, shards, place, 0)


def flatten(grads, plan, shards):
    vmem = pl.BlockSpec(memory_space=pltpu.VMEM)
    return pl.pallas_call(
        functools.partial(flatten_kernel, plan, shards),
        out_shape=jax.ShapeDtypeStruct((shards, plan["span"], LANES), bf16),
        in_specs=[pl.BlockSpec(memory_space=pltpu.SMEM)] + [vmem] * len(layout()),
        out_specs=vmem,
        scratch_shapes=[
            pltpu.VMEM((plan["height"], LANES), f32),
            pltpu.VMEM((5, MS, LANES), f32),
        ],
        name="flatten",
    )(jnp.asarray(plan["bases"], jnp.int32), *[grads[label] for label, shape in layout()])


def ln_parts(value):
    mean = jnp.mean(value, -1, keepdims=True)
    centred = value - mean
    variance = jnp.mean(centred * centred, -1, keepdims=True)
    inverse = lax.rsqrt(variance + norm_eps)
    return centred * inverse, inverse


def ln_back(grad, hat, inverse, gain):
    scaled = grad * gain
    first = jnp.mean(scaled, -1, keepdims=True)
    second = jnp.mean(scaled * hat, -1, keepdims=True)
    return inverse * (scaled - first - hat * second)


def gelu_parts(value):
    cdf = 0.5 + 0.5 * lax.erf(value * (2.0**-0.5))
    density = jnp.exp(value * value * -0.5) * (1.0 / math.sqrt(2.0 * math.pi))
    return value * cdf, cdf + value * density


def col_sum(value):
    return jnp.sum(value, 0, keepdims=True)


def groups(width):
    size = width // HEADS
    found = []
    for start in range(0, width, LANES):
        stop = min(start + LANES, width)
        found.append((start, stop, (stop - start) // size))
    return found, size


def stack_heads(value, count, size):
    lane = lax.broadcasted_iota(jnp.int32, value.shape, 1)
    zero = jnp.zeros_like(value)
    return jnp.concatenate(
        [
            jnp.where((lane >= head * size) & (lane < (head + 1) * size), value, zero)
            for head in range(count)
        ],
        0,
    )


def merge_heads(value, count, size):
    rows = value.shape[0] // count
    lane = lax.broadcasted_iota(jnp.int32, (rows, value.shape[1]), 1)
    merged = value[0:rows]
    for head in range(1, count):
        merged = jnp.where(lane >= head * size, value[head * rows : (head + 1) * rows], merged)
    return merged


def forward_kernel(
    pair,
    length,
    tall,
    chunk,
    tok_ref,
    ln1_ref,
    qkv_w,
    qkv_b,
    proj_w,
    proj_b,
    ln2_ref,
    fc1_w,
    fc1_b,
    fc2_w,
    fc2_b,
    to_ln,
    to_w,
    to_b,
    a1_ref,
    qkv_ref,
    probs_ref,
    att_ref,
    mid_ref,
    n2_ref,
    z_ref,
    slope_ref,
    y_ref,
    sent_ref,
    head_ref,
):
    step = pl.program_id(0)
    rows = pair * tall
    width = tok_ref.shape[-1]
    hidden = fc1_w.shape[1]
    found, size = groups(width)
    scale = size ** (-0.5)
    tokens = tok_ref[...].reshape(rows, width).astype(f32)
    hat, _ = ln_parts(tokens)
    a1 = (hat * ln1_ref[0:1, :] + ln1_ref[1:2, :]).astype(bf16)
    a1_ref[...] = a1
    qkv_ref[...] = (mm(a1, qkv_w[...]) + qkv_b[...]).astype(bf16)
    key_lane = lax.broadcasted_iota(jnp.int32, (1, tall), 1)
    bias = jnp.where(key_lane < length, 0.0, -1e30).astype(f32)
    for crop in range(pair):
        here = slice(crop * tall, (crop + 1) * tall)
        for start, stop, count in found:
            query = stack_heads(qkv_ref[here, start:stop], count, size)
            key = qkv_ref[here, width + start : width + stop]
            value = qkv_ref[here, 2 * width + start : 2 * width + stop]
            scores = mm_t(query, key) * scale + bias
            summit = jnp.max(scores, -1, keepdims=True)
            weights = jnp.exp(scores - summit)
            probs = (weights / jnp.sum(weights, -1, keepdims=True)).astype(bf16)
            first = start // size
            for head in range(count):
                probs_ref[crop, first + head] = probs[head * tall : (head + 1) * tall]
            att_ref[here, start:stop] = merge_heads(mm(probs, value), count, size).astype(bf16)
    mid = tokens + mm(att_ref[...], proj_w[...]) + proj_b[...]
    mid_ref[...] = mid
    hat, _ = ln_parts(mid)
    n2_ref[...] = (hat * ln2_ref[0:1, :] + ln2_ref[1:2, :]).astype(bf16)
    y_ref[...] = mid + fc2_b[...]
    for number in range(hidden // chunk):
        cols = slice(number * chunk, (number + 1) * chunk)
        inner = mm(n2_ref[...], fc1_w[:, cols]) + fc1_b[:, cols]
        active, slope = gelu_parts(inner)
        z_ref[:, cols] = active.astype(bf16)
        slope_ref[:, cols] = slope.astype(bf16)
        y_ref[...] += mm(z_ref[:, cols], fc2_w[cols, :])
    for crop in range(pair):
        head_ref[pl.ds(step * pair + crop, 1), :] = y_ref[crop * tall : crop * tall + 1, :]

    @pl.when(step == pl.num_programs(0) - 1)
    def _():
        hat, _ = ln_parts(head_ref[...])
        active, _ = gelu_parts(hat * to_ln[0:1, :] + to_ln[1:2, :])
        sent_ref[...] = (mm(active.astype(bf16), to_w[...]) + to_b[...]).astype(bf16)


def block_forward(tokens, params, label, length, pair):
    crops, tall, width = tokens.shape
    hidden = params[label + "_fc1_w"].shape[1]
    other = params[label + "_to_w"].shape[1]
    rows = pair * tall
    names = ("ln1", "qkv_w", "qkv_b", "proj_w", "proj_b", "ln2", "fc1_w", "fc1_b", "fc2_w", "fc2_b")
    names = names + ("to_ln", "to_w", "to_b")
    weights = [params[label + "_" + name] for name in names]
    flat = crops * tall

    def by_rows(cols):
        return pl.BlockSpec((rows, cols), lambda i: (i, 0))

    outs = [
        (by_rows(width), jax.ShapeDtypeStruct((flat, width), bf16)),
        (by_rows(3 * width), jax.ShapeDtypeStruct((flat, 3 * width), bf16)),
        (
            pl.BlockSpec((pair, HEADS, tall, tall), lambda i: (i, 0, 0, 0)),
            jax.ShapeDtypeStruct((crops, HEADS, tall, tall), bf16),
        ),
        (by_rows(width), jax.ShapeDtypeStruct((flat, width), bf16)),
        (by_rows(width), jax.ShapeDtypeStruct((flat, width), f32)),
        (by_rows(width), jax.ShapeDtypeStruct((flat, width), bf16)),
        (by_rows(hidden), jax.ShapeDtypeStruct((flat, hidden), bf16)),
        (by_rows(hidden), jax.ShapeDtypeStruct((flat, hidden), bf16)),
        (by_rows(width), jax.ShapeDtypeStruct((flat, width), f32)),
        (
            pl.BlockSpec((crops, other), lambda i: (0, 0)),
            jax.ShapeDtypeStruct((crops, other), bf16),
        ),
        (
            pl.BlockSpec((crops, width), lambda i: (0, 0)),
            jax.ShapeDtypeStruct((crops, width), f32),
        ),
    ]
    flops = 2 * flat * (4 * width * width + 2 * width * hidden)
    return pl.pallas_call(
        functools.partial(forward_kernel, pair, length, tall, 384),
        grid=(crops // pair,),
        out_shape=[shape for spec, shape in outs],
        in_specs=[pl.BlockSpec((pair, tall, width), lambda i: (i, 0, 0))]
        + [whole(value.shape) for value in weights],
        out_specs=[spec for spec, shape in outs],
        cost_estimate=estimate(flops, 20_000_000),
        name="forward_" + label,
    )(tokens, *weights)


def cross_kernel(
    length,
    tall,
    crops,
    sent_ref,
    y_ref,
    gret_ref,
    ca_ln,
    q_w,
    q_b,
    k_w,
    v_w,
    v_b,
    o_w,
    o_b,
    back_ln,
    back_w,
    back_b,
    returned_ref,
    gsent_ref,
    gj_ref,
    d_ca_ln,
    d_q_w,
    d_q_b,
    d_k_w,
    d_v_w,
    d_v_b,
    d_o_w,
    d_o_b,
    d_back_ln,
    d_back_w,
    d_back_b,
    sent_f,
    n_all,
    k_all,
    v_all,
    gk_all,
    gv_all,
    query_all,
    probs_all,
    att_all,
    gatt_all,
    gq_all,
    gn_head,
    gj_head,
):
    width = y_ref.shape[1]
    size = width // HEADS
    scale = size ** (-0.5)
    lane = lax.broadcasted_iota(jnp.int32, (8, width), 1)
    head = lax.broadcasted_iota(jnp.int32, (8, width), 0)
    own_head = (lane >= head * size) & (lane < (head + 1) * size)
    row = lax.broadcasted_iota(jnp.int32, (tall, 1), 0)
    key_lane = lax.broadcasted_iota(jnp.int32, (1, tall), 1)
    bias = jnp.where(key_lane < length, 0.0, -1e30).astype(f32)
    gain, shift = ca_ln[0:1, :], ca_ln[1:2, :]
    sent_f[...] = sent_ref[...].astype(f32)
    hat, _ = ln_parts(sent_f[...])
    n_head = (hat * gain + shift).astype(bf16)
    query_all[...] = (mm(n_head, q_w[...]) + q_b[...]).astype(bf16).astype(f32)

    def joined(crop):
        here = pl.ds(pl.multiple_of(crop * tall, 16), tall)
        return here, jnp.where(row == 0, sent_f[pl.ds(crop, 1), :], y_ref[here, :])

    def spread(ref, crop):
        return jnp.where(own_head, ref[pl.ds(crop, 1), :], 0.0).astype(bf16)

    def ahead(crop, carry):
        here, value = joined(crop)
        hat, _ = ln_parts(value)
        normed = (hat * gain + shift).astype(bf16)
        n_all[here, :] = normed
        key = mm(normed, k_w[...]).astype(bf16)
        k_all[here, :] = key
        vals = (mm(normed, v_w[...]) + v_b[...]).astype(bf16)
        v_all[here, :] = vals
        scores = mm_t(spread(query_all, crop), key) * scale + bias
        summit = jnp.max(scores, -1, keepdims=True)
        weights = jnp.exp(scores - summit)
        probs = weights / jnp.sum(weights, -1, keepdims=True)
        probs_all[crop] = probs
        mixed = jnp.where(own_head, mm(probs.astype(bf16), vals), 0.0)
        att_all[pl.ds(crop, 1), :] = col_sum(mixed)
        return carry

    lax.fori_loop(0, crops, ahead, 0)
    attended = att_all[...].astype(bf16)
    merged = sent_f[...] + mm(attended, o_w[...]) + o_b[...]
    hat, inverse = ln_parts(merged)
    active, slope = gelu_parts(hat * back_ln[0:1, :] + back_ln[1:2, :])
    active = active.astype(bf16)
    returned_ref[...] = (mm(active, back_w[...]) + back_b[...]).astype(bf16)
    gret = gret_ref[...]
    d_back_w[...] = t_mm(active, gret)
    d_back_b[...] = col_sum(gret.astype(f32))
    gact = mm_t(gret, back_w[...]) * slope
    d_back_ln[0:1, :] = col_sum(gact * hat)
    d_back_ln[1:2, :] = col_sum(gact)
    gfused = ln_back(gact, hat, inverse, back_ln[0:1, :])
    gfo = gfused.astype(bf16)
    d_o_w[...] = t_mm(attended, gfo)
    d_o_b[...] = col_sum(gfo.astype(f32))
    gatt_all[...] = mm_t(gfo, o_w[...]).astype(bf16).astype(f32)

    def behind(crop, carry):
        here = pl.ds(pl.multiple_of(crop * tall, 16), tall)
        probs = probs_all[crop]
        gatt = spread(gatt_all, crop)
        gprobs = mm_t(gatt, v_all[here, :])
        gv_all[here, :] = t_mm(probs.astype(bf16), gatt).astype(bf16)
        inner = gprobs - jnp.sum(gprobs * probs, -1, keepdims=True)
        gscores = (probs * inner).astype(bf16)
        gq = jnp.where(own_head, mm(gscores, k_all[here, :]), 0.0)
        gq_all[pl.ds(crop, 1), :] = col_sum(gq) * scale
        gk_all[here, :] = (t_mm(gscores, spread(query_all, crop)) * scale).astype(bf16)
        return carry

    lax.fori_loop(0, crops, behind, 0)
    gq = gq_all[...].astype(bf16)
    d_q_w[...] = t_mm(n_head, gq)
    d_q_b[...] = col_sum(gq.astype(f32))
    gn_head[...] = mm_t(gq, q_w[...])
    d_ca_ln[...] = jnp.zeros_like(d_ca_ln)
    d_v_b[...] = jnp.zeros_like(d_v_b)
    d_k_w[...] = jnp.zeros_like(d_k_w)
    d_v_w[...] = jnp.zeros_like(d_v_w)

    def finish(crop, carry):
        here, value = joined(crop)
        hat, inverse = ln_parts(value)
        gk, gv = gk_all[here, :], gv_all[here, :]
        gn = mm_t(gk, k_w[...]) + mm_t(gv, v_w[...])
        gn = gn + jnp.where(row == 0, gn_head[pl.ds(crop, 1), :], 0.0)
        d_ca_ln[0:1, :] += col_sum(gn * hat)
        d_ca_ln[1:2, :] += col_sum(gn)
        gj = ln_back(gn, hat, inverse, gain)
        gj_ref[here, :] = gj
        gj_head[pl.ds(crop, 1), :] = gj[0:1, :]
        d_v_b[...] += col_sum(gv.astype(f32))
        return carry

    lax.fori_loop(0, crops, finish, 0)
    gsent_ref[...] = (gj_head[...] + gfused).astype(bf16)

    def weights_of(pair, carry):
        here = pl.ds(pl.multiple_of(pair * 2 * tall, 32), 2 * tall)
        normed = n_all[here, :]
        d_k_w[...] += t_mm(normed, gk_all[here, :])
        d_v_w[...] += t_mm(normed, gv_all[here, :])
        return carry

    lax.fori_loop(0, crops // 2, weights_of, 0)


def cross(sent, hosted, gret, params, label, length, tall):
    crops, width = sent.shape
    own = gret.shape[1]
    flat = crops * tall
    names = ("ca_ln", "ca_q_w", "ca_q_b", "ca_k_w", "ca_v_w", "ca_v_b", "ca_o_w", "ca_o_b")
    names = names + ("back_ln", "back_w", "back_b")
    weights = [params[label + "_" + name] for name in names]
    outs = [
        jax.ShapeDtypeStruct((crops, own), bf16),
        jax.ShapeDtypeStruct((crops, width), bf16),
        jax.ShapeDtypeStruct((flat, width), f32),
    ] + [jax.ShapeDtypeStruct(value.shape, f32) for value in weights]
    vmem = pl.BlockSpec(memory_space=pltpu.VMEM)
    small = pltpu.VMEM((crops, width), f32)
    big = pltpu.VMEM((flat, width), bf16)
    values = pl.pallas_call(
        functools.partial(cross_kernel, length, tall, crops),
        out_shape=outs,
        in_specs=[vmem] * (3 + len(weights)),
        out_specs=[vmem] * len(outs),
        scratch_shapes=[small]
        + [big] * 5
        + [small, pltpu.VMEM((crops, 8, tall), f32)]
        + [small] * 5,
        cost_estimate=estimate(2 * flat * width * width * 6, 8_000_000),
        name="cross_" + label,
    )(sent, hosted, gret, *weights)
    grads = {label + "_" + name: value for name, value in zip(names, values[3:])}
    return values[0], values[1], values[2], grads


def backward_kernel(
    pair,
    length,
    tall,
    chunk,
    live_ref,
    tok_ref,
    cot_ref,
    y_ref,
    gj_ref,
    a1_ref,
    qkv_ref,
    probs_ref,
    att_ref,
    mid_ref,
    n2_ref,
    z_ref,
    slope_ref,
    headrow_ref,
    gsent_ref,
    returned_ref,
    ln1_ref,
    qkv_w,
    proj_w,
    ln2_ref,
    fc1_w,
    fc2_w,
    to_ln,
    to_w,
    out_ref,
    gtok_ref,
    d_ln1,
    d_qkv_w,
    d_qkv_b,
    d_proj_w,
    d_proj_b,
    d_ln2,
    d_fc1_w,
    d_fc1_b,
    d_fc2_w,
    d_fc2_b,
    d_to_ln,
    d_to_w,
    d_to_b,
    ghead,
    gy,
    gnormed,
    gqkv,
    gatt_ref,
):
    step = pl.program_id(0)
    rows = pair * tall
    width = tok_ref.shape[-1]
    hidden = fc1_w.shape[1]
    found, size = groups(width)
    scale = size ** (-0.5)

    @pl.when(step == 0)
    def _():
        hat, inverse = ln_parts(headrow_ref[...])
        active, slope = gelu_parts(hat * to_ln[0:1, :] + to_ln[1:2, :])
        gsent = gsent_ref[...]
        d_to_w[...] = t_mm(active.astype(bf16), gsent)
        d_to_b[...] = col_sum(gsent.astype(f32))
        gact = mm_t(gsent, to_w[...]) * slope
        d_to_ln[0:1, :] = col_sum(gact * hat)
        d_to_ln[1:2, :] = col_sum(gact)
        ghead[...] = ln_back(gact, hat, inverse, to_ln[0:1, :])
        for ref in (d_ln1, d_qkv_w, d_qkv_b, d_proj_w, d_proj_b, d_ln2):
            ref[...] = jnp.zeros_like(ref)
        for ref in (d_fc1_w, d_fc1_b, d_fc2_w, d_fc2_b):
            ref[...] = jnp.zeros_like(ref)

    row = lax.broadcasted_iota(jnp.int32, (tall, 1), 0)
    for crop in range(pair):
        here = slice(crop * tall, (crop + 1) * tall)
        slot = step * pair + crop
        live = jnp.where(slot < live_ref[0], 1.0, 0.0).astype(f32)
        seed = cot_ref[crop].astype(f32) * live + gj_ref[here, :]
        gy[here, :] = jnp.where(row == 0, ghead[pl.ds(slot, 1), :], seed)
        home = returned_ref[pl.ds(slot, 1), :]
        final = jnp.where(row == 0, home, y_ref[here, :])
        out_ref[0, crop] = final[0:length].astype(bf16)
    gm = gy[...].astype(bf16)
    d_fc2_b[...] += col_sum(gm.astype(f32))
    for number in range(hidden // chunk):
        cols = slice(number * chunk, (number + 1) * chunk)
        d_fc2_w[cols, :] += t_mm(z_ref[:, cols], gm)
        gu = slope_ref[:, cols].astype(f32) * mm_t(gm, fc2_w[cols, :])
        gu = gu.astype(bf16)
        d_fc1_w[:, cols] += t_mm(n2_ref[...], gu)
        d_fc1_b[:, cols] += col_sum(gu.astype(f32))
        part = mm_t(gu, fc1_w[:, cols])
        gnormed[...] = part if number == 0 else gnormed[...] + part
    hat, inverse = ln_parts(mid_ref[...])
    gn = gnormed[...]
    d_ln2[0:1, :] += col_sum(gn * hat)
    d_ln2[1:2, :] += col_sum(gn)
    gmid = gy[...] + ln_back(gn, hat, inverse, ln2_ref[0:1, :])
    gy[...] = gmid
    gp = gmid.astype(bf16)
    d_proj_w[...] += t_mm(att_ref[...], gp)
    d_proj_b[...] += col_sum(gp.astype(f32))
    gatt_ref[...] = mm_t(gp, proj_w[...]).astype(bf16)
    for crop in range(pair):
        here = slice(crop * tall, (crop + 1) * tall)
        for start, stop, count in found:
            first = start // size
            query = stack_heads(qkv_ref[here, start:stop], count, size)
            key = qkv_ref[here, width + start : width + stop]
            value = qkv_ref[here, 2 * width + start : 2 * width + stop]
            gatt = stack_heads(gatt_ref[here, start:stop], count, size)
            probs_low = jnp.concatenate([probs_ref[crop, first + head] for head in range(count)], 0)
            probs = probs_low.astype(f32)
            gprobs = mm_t(gatt, value)
            inner = gprobs - jnp.sum(gprobs * probs, -1, keepdims=True)
            gscores = (probs * inner).astype(bf16)
            gq = merge_heads(mm(gscores, key), count, size) * scale
            gk = t_mm(gscores, query) * scale
            gv = t_mm(probs_low, gatt)
            gqkv[here, start:stop] = gq.astype(bf16)
            gqkv[here, width + start : width + stop] = gk.astype(bf16)
            gqkv[here, 2 * width + start : 2 * width + stop] = gv.astype(bf16)
    grad = gqkv[...]
    d_qkv_w[...] += t_mm(a1_ref[...], grad)
    d_qkv_b[...] += col_sum(grad.astype(f32))
    gn = mm_t(grad, qkv_w[...])
    hat, inverse = ln_parts(tok_ref[...].reshape(rows, width).astype(f32))
    d_ln1[0:1, :] += col_sum(gn * hat)
    d_ln1[1:2, :] += col_sum(gn)
    gtok = gy[...] + ln_back(gn, hat, inverse, ln1_ref[0:1, :])
    for crop in range(pair):
        gtok_ref[0, crop] = gtok[crop * tall : crop * tall + length].astype(bf16)


def block_backward(tokens, cot, live, kept, gj, gsent, returned, params, label, length, pair):
    crops, tall, width = tokens.shape
    a1, qkv, probs, att, mid, n2, z, slope, y, headrow = kept
    hidden = params[label + "_fc1_w"].shape[1]
    rows = pair * tall
    flat = crops * tall
    names = ("ln1", "qkv_w", "proj_w", "ln2", "fc1_w", "fc2_w", "to_ln", "to_w")
    weights = [params[label + "_" + name] for name in names]

    def by_rows(cols):
        return pl.BlockSpec((rows, cols), lambda i: (i, 0))

    token_spec = pl.BlockSpec((pair, tall, width), lambda i: (i, 0, 0))
    out_spec = pl.BlockSpec((1, pair, length, width), lambda i: (0, i, 0, 0))
    grad_names = (
        "ln1",
        "qkv_w",
        "qkv_b",
        "proj_w",
        "proj_b",
        "ln2",
        "fc1_w",
        "fc1_b",
        "fc2_w",
        "fc2_b",
        "to_ln",
        "to_w",
        "to_b",
    )
    grad_shapes = [params[label + "_" + name].shape for name in grad_names]
    out_shape = jax.ShapeDtypeStruct((1, crops, length, width), bf16)
    returned = returned.astype(f32)
    values = pl.pallas_call(
        functools.partial(backward_kernel, pair, length, tall, 384),
        grid=(crops // pair,),
        out_shape=[out_shape, out_shape] + [jax.ShapeDtypeStruct(s, f32) for s in grad_shapes],
        in_specs=[
            pl.BlockSpec(memory_space=pltpu.SMEM),
            token_spec,
            token_spec,
            by_rows(width),
            by_rows(width),
            by_rows(width),
            by_rows(3 * width),
            pl.BlockSpec((pair, HEADS, tall, tall), lambda i: (i, 0, 0, 0)),
            by_rows(width),
            by_rows(width),
            by_rows(width),
            by_rows(hidden),
            by_rows(hidden),
            whole(headrow.shape),
            whole(gsent.shape),
            whole(returned.shape),
        ]
        + [whole(value.shape) for value in weights],
        out_specs=[out_spec, out_spec] + [pl.BlockSpec(s, lambda i: (0, 0)) for s in grad_shapes],
        scratch_shapes=[
            pltpu.VMEM((crops, width), f32),
            pltpu.VMEM((rows, width), f32),
            pltpu.VMEM((rows, width), f32),
            pltpu.VMEM((rows, 3 * width), bf16),
            pltpu.VMEM((rows, width), bf16),
        ],
        cost_estimate=estimate(4 * flat * (4 * width * width + 2 * width * hidden), 30_000_000),
        name="backward_" + label,
    )(
        live,
        tokens,
        cot,
        y,
        gj,
        a1,
        qkv,
        probs,
        att,
        mid,
        n2,
        z,
        slope,
        headrow,
        gsent,
        returned,
        *weights,
    )
    grads = {label + "_" + name: value for name, value in zip(grad_names, values[2:])}
    return values[0], values[1], grads


def swap(value):
    return lax.ppermute(value, "branch", [(0, 1), (1, 0)])


def partner(value, bit):
    count = lax.axis_size("dp")
    return lax.ppermute(value, "dp", [(i, i ^ bit) for i in range(count)])


def shards(
    small_tokens,
    large_tokens,
    small_cot,
    large_cot,
    live_counts,
    master,
    first_moment,
    second_moment,
):
    count = lax.axis_size("branch") * lax.axis_size("dp")
    plan = grid_plan(count)
    index = lax.axis_index(("branch", "dp"))
    size = master.shape[0]
    rows = plan["shard_rows"]
    table = lax.dynamic_index_in_dim(jnp.asarray(plan["table"]), index, 0, False)
    padded = jnp.pad(master, (0, rows * LANES - size)).reshape(rows, LANES)
    own = align(padded, table, plan)
    grid = lax.all_gather(own, ("branch", "dp"), axis=0, tiled=False)
    params = unflatten(grid, plan, count)

    half = lax.axis_index("branch")
    counts = live_counts[:, 0]
    own_count = lax.dynamic_slice_in_dim(counts, half, 1)
    far_count = lax.dynamic_slice_in_dim(counts, 1 - half, 1)
    crops, length_s = small_tokens.shape[1], small_tokens.shape[2]
    length_l = large_tokens.shape[2]
    tall_s, tall_l = round_up(length_s, 16), round_up(length_l, 16)
    pair = 2

    def taller(value, length, tall):
        return jnp.pad(value[0], ((0, 0), (0, tall - length), (0, 0)))

    small = taller(small_tokens, length_s, tall_s)
    large = taller(large_tokens, length_l, tall_l)
    small_seed = taller(small_cot, length_s, tall_s)
    large_seed = taller(large_cot, length_l, tall_l)
    slots = jnp.arange(crops, dtype=jnp.int32)[:, None]
    ret_small = jnp.where(slots < own_count, small_cot[0, :, 0], 0)
    ret_large = jnp.where(slots < far_count, large_cot[0, :, 0], 0)
    ret_small, ret_large = swap(ret_small), swap(ret_large)

    *kept_s, sent_s, head_s = block_forward(small, params, "s", length_s, pair)
    got_s = swap(sent_s)
    *kept_l, sent_l, head_l = block_forward(large, params, "l", length_l, pair)
    got_l = swap(sent_l)
    grads = {}
    back_s, gsent_s, gj_l, part = cross(got_s, kept_l[-1], ret_small, params, "s", length_l, tall_l)
    grads.update(part)
    home_s, own_s = swap(back_s), swap(gsent_s)
    back_l, gsent_l, gj_s, part = cross(got_l, kept_s[-1], ret_large, params, "l", length_s, tall_s)
    grads.update(part)
    home_l, own_l = swap(back_l), swap(gsent_l)
    small_out, small_grad, part = block_backward(
        small, small_seed, own_count, (*kept_s, head_s), gj_s, own_s, home_s, params, "s", length_s, pair
    )
    grads.update(part)
    large_out, large_grad, part = block_backward(
        large, large_seed, far_count, (*kept_l, head_l), gj_l, own_l, home_l, params, "l", length_l, pair
    )
    grads.update(part)

    flat = flatten(grads, plan, count)
    mine = lax.psum_scatter(flat, ("branch", "dp"), scatter_dimension=0, tiled=False)
    summed, square = unalign(mine.astype(f32), table, plan)
    square = square + swap(square)
    bit = 1
    while bit < lax.axis_size("dp"):
        square = square + partner(square, bit)
        bit *= 2
    grad_norm = jnp.sqrt(square[0, 0])
    own_grad = summed.reshape(-1)[:size]
    clipped = own_grad * jnp.minimum(1.0, clip_norm / grad_norm)
    new_first = beta_one * first_moment + (1.0 - beta_one) * clipped
    new_second = beta_two * second_moment + (1.0 - beta_two) * clipped * clipped
    new_master = master - rate * (
        new_first / bias_one / (jnp.sqrt(new_second / bias_two) + adam_eps) + decay * master
    )
    return (
        small_out,
        large_out,
        small_grad,
        large_grad,
        grad_norm,
        new_first,
        new_second,
        new_master,
        new_master.astype(bf16),
    )


def solution(mesh):
    return jax.shard_map(
        shards,
        mesh=mesh,
        in_specs=(
            P("branch", "dp", None, None),
            P("branch", "dp", None, None),
            P("branch", "dp", None, None),
            P("branch", "dp", None, None),
            P(None, "dp"),
            P(("branch", "dp")),
            P(("branch", "dp")),
            P(("branch", "dp")),
        ),
        out_specs=(
            P("branch", "dp", None, None),
            P("branch", "dp", None, None),
            P("branch", "dp", None, None),
            P("branch", "dp", None, None),
            P(),
            P(("branch", "dp")),
            P(("branch", "dp")),
            P(("branch", "dp")),
            P(("branch", "dp")),
        ),
        check_vma=False,
    )
```

time: 1090 us -> 411 us (0.38); the launches traced: 1070 us -> 410 us
  local copies, waits for them, and re-layouts: 346 us -> 17.7 us
  waiting for transfers between devices: 371 us -> 188 us
  matrix products: 174 us -> 0 us
  Pallas kernels: 0 us -> 173 us
  other arithmetic: 158 us -> 7.11 us
    psum x1 -> x0, waiting for transfers between devices: 219 us -> none  [shards(): summed = lax.psum(flat_grad, ('branch', 'dp'))]
    dot_general x80 -> x0, matrix products: 174 us -> none  [the longest x20 40.9 us: product_back(): lax.dot_general(grad, right, (((grad.ndim - 1,), (1,)), ((), ())), prefer...]
    pallas_call x0 -> x10, Pallas kernels: none -> 173 us  [the longest x2 65.1 us: block_backward(): pl.pallas_call(functools.partial(backward_kernel, pair, length, tall, 384...]
    unnamed x3 -> x2, waiting for transfers between devices: 151 us -> 0.03 us
    concatenate x4 -> x0, local copies, waits for them, and re-layouts: 150 us -> none  [the longest x1 146 us: shards(): jnp.concatenate([grads[label].reshape(-1) for label, shape in layout()])]
    reduce_scatter x0 -> x1, waiting for transfers between devices: none -> 117 us  [shards(): lax.psum_scatter(flat, ('branch', 'dp'), scatter_dimension=0, tiled=False)]
    convert_element_type x26 -> x4, other arithmetic: 72.5 us -> 4.22 us  [the longest x1 1.71 us: shards(): summed, square = unalign(mine.astype(f32), table, plan)]
    reshape x64 -> x1, local copies, waits for them, and re-layouts: 68.9 us -> 1.87 us  [shards(): padded = jnp.pad(master, (0, rows * LANES - size)).reshape(rows, LANES)]
  transfers between devices with their start and end apart: 10 -> 15, of which waited for: 2 -> 6; matrix products, arithmetic and copies ran while one was open for 20% -> 3% of each run, Pallas kernels for 0% -> 33%
where the time goes in v1:
time: 411 us; the launch traced here: 410 us
  waiting for transfers between devices  188 us (46%)
  Pallas kernels  173 us (42%)
  local copies, waits for them, and re-layouts  17.7 us (4%)
  between operations  16.2 us (4%)
  starting transfers between devices  7.99 us (2%)
  other arithmetic  7.11 us (2%)
    reduce_scatter x1, waiting for transfers between devices, shards(): lax.psum_scatter(flat, ('branch', 'dp'), scatter_dimension=0, tiled=False)  117 us
    pallas_call x2, Pallas kernels, block_backward(): pl.pallas_call(functools.partial(backward_kernel, pair, length, tall, 384...  65.1 us
    all_gather x1, waiting for transfers between devices, shards(): grid = lax.all_gather(own, ('branch', 'dp'), axis=0, tiled=False)  63.2 us
    pallas_call x2, Pallas kernels, block_forward(): pl.pallas_call(functools.partial(forward_kernel, pair, length, tall, 384)...  43.3 us
    pallas_call x2, Pallas kernels, cross(): pl.pallas_call(functools.partial(cross_kernel, length, tall, crops), out_...  42.1 us
    pallas_call x1, Pallas kernels, flatten(): pl.pallas_call(functools.partial(flatten_kernel, plan, shards), out_shape...  10 us
    unnamed x44, local copies, waits for them, and re-layouts  9.14 us
  transfers between devices with their start and end apart: 15, of which 6 were waited for; matrix products, arithmetic and copies ran while one was open for 3% of the time, Pallas kernels for 33%

profile of v1, /device:TPU:0, one launch (start us, length us, event | category | flops | bytes accessed | tf_op | source)
XLA Modules:
  0.0 410.0 jit_solution(9031008832462327511)
XLA Ops:
  7.2 1.9 pad_bitcast_fusion.shard_ref
  9.1 1.3 fusion.1.table_ref
  10.4 2.3 align.1
  16.2 1.2 copy.34
  18.6 0.9 pad.18.tok_ref
  19.5 1.0 pad.19.cot_ref
  20.6 1.2 pad.21.tok_ref
  21.8 1.2 pad.22.cot_ref
  23.0 63.2 %all-gather.3.cloned.1.call-done = bf16[26112,128]{1,0:T(8,128)(2,1)} async-done(((bf16[816,128]{1,0:T(8,128)(2,1)}), bf16[26112,128]{1,0:T(8,128)(2,1)}) %all-gather.3.cloned.1.call-update) | async-done | bytes 6684688 | tf_op jit(solution)/shard_map/all_gather | solution.py:1025
  86.2 7.7 %unflatten.1 = (f32[2,192]{1,0:T(2,128)}, bf16[192,576]{1,0:T(8,128)(2,1)}, f32[1,576]{1,0:T(1,128)}, bf16[192,192]{1,0:T(8,128)(2,1)}, f32[1,192]{1,0:T(1,128)}...) custom-call(s32[32]{0:T(128)} %constant.47.clone.base_ref, ...), custom_call_target="tpu_custom_call" | custom-call | tf_op jit(solution)/shard_map/unflatten/pallas_call | solution.py:360
  93.8 28.3 %forward_l.1 = (bf16[1664,384]{1,0:T(8,128)(2,1)}, bf16[1664,1152]{1,0:T(8,128)(2,1)}, bf16[8,6,208,208]{3,2,1,0:T(8,128)(2,1)}, bf16[1664,384]{1,0:T(8,128)(2,1...) custom-call(bf16[8,208,384]{2,1,0:T(8,128)(2,1)} %pad.21.tok_ref, ...), custom_call_target="tpu_custom_call" | custom-call | flops 5888802816 | bytes 20000000 | tf_op jit(solution)/shard_map/forward_l/pallas_call | solution.py:577
  122.5 15.0 %forward_s.1 = (bf16[1280,192]{1,0:T(8,128)(2,1)}, bf16[1280,576]{1,0:T(8,128)(2,1)}, bf16[8,6,160,160]{3,2,1,0:T(8,128)(2,1)}, bf16[1280,192]{1,0:T(8,128)(2,1)...) custom-call(bf16[8,160,192]{2,1,0:T(8,128)(2,1)} %pad.18.tok_ref, ...), custom_call_target="tpu_custom_call" | custom-call | flops 1132462080 | bytes 20000000 | tf_op jit(solution)/shard_map/forward_s/pallas_call | solution.py:577
  138.5 17.7 %cross_l.1 = (bf16[8,384]{1,0:T(8,128)(2,1)}, bf16[8,192]{1,0:T(8,128)(2,1)}, f32[1280,192]{1,0:T(8,128)}, f32[2,192]{1,0:T(2,128)}, f32[192,192]{1,0:T(8,128)},...) custom-call(bf16[8,192]{1,0:T(8,128)(2,1)} %copy-done.17, ...), custom_call_target="tpu_custom_call" | custom-call | flops 566231040 | bytes 8000000 | tf_op jit(solution)/shard_map/cross_l/pallas_call | solution.py:759
  157.3 24.4 %cross_s.1 = (bf16[8,192]{1,0:T(8,128)(2,1)}, bf16[8,384]{1,0:T(8,128)(2,1)}, f32[1664,384]{1,0:T(8,128)}, f32[2,384]{1,0:T(2,128)}, f32[384,384]{1,0:T(8,128)},...) custom-call(bf16[8,384]{1,0:T(8,128)(2,1)} %copy-done.14, ...), custom_call_target="tpu_custom_call" | custom-call | flops 2944401408 | bytes 8000000 | tf_op jit(solution)/shard_map/cross_s/pallas_call | solution.py:759
  183.6 43.2 %backward_l.1 = (bf16[1,8,197,384]{3,2,1,0:T(8,128)(2,1)}, bf16[1,8,197,384]{3,2,1,0:T(8,128)(2,1)}, f32[2,384]{1,0:T(2,128)}, f32[384,1152]{1,0:T(8,128)}, f32[...) custom-call(s32[1]{0:T(128)} %bitcast.11.live_ref, ...), custom_call_target="tpu_custom_call" | custom-call | flops 11777605632 | bytes 30000000 | tf_op jit(solution)/shard_map/backward_l/pallas_call | solution.py:942
  227.9 22.0 %backward_s.1 = (bf16[1,8,145,192]{3,2,1,0:T(8,128)(2,1)}, bf16[1,8,145,192]{3,2,1,0:T(8,128)(2,1)}, f32[2,192]{1,0:T(2,128)}, f32[192,576]{1,0:T(8,128)}, f32[1...) custom-call(s32[1]{0:T(128)} %bitcast.live_ref, ...), custom_call_target="tpu_custom_call" | custom-call | flops 2264924160 | bytes 30000000 | tf_op jit(solution)/shard_map/backward_s/pallas_call | solution.py:942
  249.9 10.0 %flatten.1 = bf16[32,816,128]{2,1,0:T(8,128)(2,1)} custom-call(s32[32]{0:T(128)} %constant.47.clone.base_ref, f32[2,192]{1,0:T(2,128)} %get-tuple-element.219.refs_0_, f32[192,576]{1,0:T(8,128)} %get-tuple-element.220.refs_1_, f32[1,576]{1,0:T(1,128)} %get-tuple-element.221.refs_2_, f32[192,192]{1,0:T(8,128)} %get-tuple-element.222.refs_3_, ...), custom_call_target="tpu_custom_call" | custom-call | tf_op jit(solution)/shard_map/flatten/pallas_call | solution.py:393
  259.9 116.7 %reduce-scatter.2.cloned.1.call-done = bf16[1,816,128]{2,1,0:T(8,128)(2,1)} async-done(((bf16[32,816,128]{2,1,0:T(8,128)(2,1)}), bf16[1,816,128]{2,1,0:T(8,128)(2,1)}) %reduce-scatter.2.cloned.1.call-update) | async-done | bytes 208912 | tf_op jit(solution)/shard_map/reduce_scatter | solution.py:1070
  376.7 1.7 bitcast_convert_fusion.grid_ref
  378.4 2.5 unalign.1
  380.9 1.4 collective-permute-done.8
  383.0 1.5 collective-permute-start.9
  384.4 2.1 collective-permute-done.9
  386.6 1.5 collective-permute-start.10
  388.1 2.1 collective-permute-done.10
  390.2 1.2 collective-permute-start.11
  391.4 2.4 collective-permute-done.11
  393.8 1.3 collective-permute-start.12
  395.1 1.2 copy.25
  396.3 1.2 copy.27
  397.5 0.9 copy.24
  400.7 1.3 fusion.2
  (75 shorter events, 12.4 us)
Async XLA Ops:
  7.2 5.6 %copy-start.12 = (s32[2,1]{0,1:T(1,128)S(1)}, s32[2,1]{0,1:T(1,128)}, u32[]{:S(2)}) copy-start(s32[2,1]{0,1:T(1,128)} %param.15) | copy-start | bytes 28
  7.2 6.9 %copy-start.3 = (bf16[1,8,197,384]{3,1,2,0:T(8,128)(2,1)S(1)}, bf16[1,8,197,384]{3,1,2,0:T(8,128)(2,1)}, u32[]{:S(2)}) copy-start(bf16[1,8,197,384]{3,1,2,0:T(8,128)(2,1)} %param.14) | copy-start | bytes 3631108
  7.2 79.0 %all-gather.3.cloned.1.call-start = ((), (), s32[]{:S(2)}) async-start(), calls=%async_computation.2 | async-start | bytes 6893568 | tf_op jit(solution)/shard_map/all_gather | solution.py:1025
  12.7 363.9 %reduce-scatter.2.cloned.1.call-start = ((), (), s32[]{:S(2)}) async-start(), calls=%async_computation.1 | async-start | bytes 6893568 | tf_op jit(solution)/shard_map/reduce_scatter | solution.py:1070
  14.2 123.7 %collective-permute-start.1 = (bf16[8,384]{1,0:T(8,128)(2,1)S(1)}, bf16[8,384]{1,0:T(8,128)(2,1)S(1)}, u32[]{:S(2)}, u32[]{:S(2)}) collective-permute-start(bf16[8,384]{1,0:T(8,128)(2,1)S(1)} %bitcast_select_fusion), channel_id=1, source_target_pairs={{0,16},{16,0},{1,17},{17,1},{2,18},{18,2},{3,19},{19,3},{4,20},{20... | collective-permute-start | bytes 18440 | tf_op jit(solution)/shard_map/ppermute | solution.py:999
  16.2 140.6 %collective-permute-start.3 = (bf16[8,192]{1,0:T(8,128)(2,1)S(1)}, bf16[8,192]{1,0:T(8,128)(2,1)S(1)}, u32[]{:S(2)}, u32[]{:S(2)}) collective-permute-start(bf16[8,192]{1,0:T(8,128)(2,1)S(1)} %bitcast_select_fusion.1), channel_id=1, source_target_pairs={{0,16},{16,0},{1,17},{17,1},{2,18},{18,2},{3,19},{19,3},{4,20},{20... | collective-permute-start | bytes 9224 | tf_op jit(solution)/shard_map/ppermute | solution.py:999
  17.4 1.1 copy-start.7
  18.6 1.9 copy-start.4
  122.2 15.7 %collective-permute-start = (bf16[8,192]{1,0:T(8,128)(2,1)}, bf16[8,192]{1,0:T(8,128)(2,1)S(1)}, u32[]{:S(2)}, u32[]{:S(2)}) collective-permute-start(bf16[8,192]{1,0:T(8,128)(2,1)} %get-tuple-element.166), channel_id=1, source_target_pairs={{0,16},{16,0},{1,17},{17,1},{2,18},{18,2},{3,19},{19,3},{4,20},{20... | collective-permute-start | bytes 9224 | tf_op jit(solution)/shard_map/ppermute | solution.py:999
  137.5 19.2 %collective-permute-start.2 = (bf16[8,384]{1,0:T(8,128)(2,1)}, bf16[8,384]{1,0:T(8,128)(2,1)S(1)}, u32[]{:S(2)}, u32[]{:S(2)}) collective-permute-start(bf16[8,384]{1,0:T(8,128)(2,1)} %get-tuple-element.188), channel_id=1, source_target_pairs={{0,16},{16,0},{1,17},{17,1},{2,18},{18,2},{3,19},{19,3},{4,20},{20... | collective-permute-start | bytes 18440 | tf_op jit(solution)/shard_map/ppermute | solution.py:999
  137.9 0.6 copy-start.17
  156.2 26.8 %collective-permute-start.6 = (bf16[8,192]{1,0:T(8,128)(2,1)}, bf16[8,192]{1,0:T(8,128)(2,1)S(1)}, u32[]{:S(2)}, u32[]{:S(2)}) collective-permute-start(bf16[8,192]{1,0:T(8,128)(2,1)} %get-tuple-element.214), channel_id=1, source_target_pairs={{0,16},{16,0},{1,17},{17,1},{2,18},{18,2},{3,19},{19,3},{4,20},{20... | collective-permute-start | bytes 9224 | tf_op jit(solution)/shard_map/ppermute | solution.py:999
  156.4 25.9 %collective-permute-start.7 = (bf16[8,384]{1,0:T(8,128)(2,1)}, bf16[8,384]{1,0:T(8,128)(2,1)S(1)}, u32[]{:S(2)}, u32[]{:S(2)}) collective-permute-start(bf16[8,384]{1,0:T(8,128)(2,1)} %get-tuple-element.215), channel_id=1, source_target_pairs={{0,16},{16,0},{1,17},{17,1},{2,18},{18,2},{3,19},{19,3},{4,20},{20... | collective-permute-start | bytes 18440 | tf_op jit(solution)/shard_map/ppermute | solution.py:999
  156.7 0.6 copy-start.15
  156.7 0.6 copy-start.14
  181.8 45.6 %collective-permute-start.4 = (bf16[8,384]{1,0:T(8,128)(2,1)}, bf16[8,384]{1,0:T(8,128)(2,1)S(1)}, u32[]{:S(2)}, u32[]{:S(2)}) collective-permute-start(bf16[8,384]{1,0:T(8,128)(2,1)} %get-tuple-element.201), channel_id=1, source_target_pairs={{0,16},{16,0},{1,17},{17,1},{2,18},{18,2},{3,19},{19,3},{4,20},{20... | collective-permute-start | bytes 18440 | tf_op jit(solution)/shard_map/ppermute | solution.py:999
  182.1 44.7 %collective-permute-start.5 = (bf16[8,192]{1,0:T(8,128)(2,1)}, bf16[8,192]{1,0:T(8,128)(2,1)S(1)}, u32[]{:S(2)}, u32[]{:S(2)}) collective-permute-start(bf16[8,192]{1,0:T(8,128)(2,1)} %get-tuple-element.202), channel_id=1, source_target_pairs={{0,16},{16,0},{1,17},{17,1},{2,18},{18,2},{3,19},{19,3},{4,20},{20... | collective-permute-start | bytes 9224 | tf_op jit(solution)/shard_map/ppermute | solution.py:999
  183.0 0.6 copy-start.16
  227.3 0.6 copy-start.11
  259.9 135.2 %copy-start.2 = (bf16[1,8,197,384]{3,2,1,0:T(8,128)(2,1)S(1)}, bf16[1,8,197,384]{3,2,1,0:T(8,128)(2,1)}, u32[]{:S(2)}) copy-start(bf16[1,8,197,384]{3,2,1,0:T(8,128)(2,1)} %get-tuple-element.270) | copy-start | bytes 3631108
  380.9 15.4 %copy-start.1 = (bf16[1,8,197,384]{3,2,1,0:T(8,128)(2,1)S(1)}, bf16[1,8,197,384]{3,2,1,0:T(8,128)(2,1)}, u32[]{:S(2)}) copy-start(bf16[1,8,197,384]{3,2,1,0:T(8,128)(2,1)} %get-tuple-element.272) | copy-start | bytes 3631108
  380.9 1.4 collective-permute-start.8
  383.0 3.6 collective-permute-start.9
  386.6 3.6 collective-permute-start.10
  390.2 3.6 collective-permute-start.11
  393.8 5.6 %collective-permute-start.12 = (f32[8,128]{1,0:T(8,128)S(1)}, f32[8,128]{1,0:T(8,128)S(1)}, u32[]{:S(2)}, u32[]{:S(2)}) collective-permute-start(f32[8,128]{1,0:T(8,128)S(1)} %add.63), channel_id=1, source_target_pairs={{0,8},{1,9},{2,10},{3,11},{4,12},{5,13},{6,14},{7,15},{8,0},{9,1},... | collective-permute-start | bytes 12296 | tf_op jit(solution)/shard_map/ppermute | solution.py:1004
  396.3 1.2 copy-start.6
  396.3 2.1 copy-start.5
  397.5 3.1 copy-start
  397.5 3.2 copy-start.8
  397.5 3.2 copy-start.9
  397.5 3.2 copy-start.10
  (1 other events, 0.6 us)
Sparse Core Ops, SparseCore 0:
  12.8 73.2 all-gather.2
  260.1 116.5 reduce-scatter.1
